TPU v7x, 32 devices: a whole 2x2x4 slice. The times are simulated.
32 devices in a mesh: dp: 8 (over y, x, core), tensor: 4 (over z).
Axes of the slice: x: 2, y: 2, z: 4, core: 2. Of those that a mesh axis runs over, the one named last changes fastest.
Arguments:
- tokens: bfloat16 [16, 577, 1024], P('dp', None, 'tensor'), may hold values from -6 to 6
- cotangent: float32 [16, 577, 1024], P('dp', None, 'tensor'), may hold values from -6 to 6
- image_counts: int32 [8], P('dp'), may hold values from 1 to 2, as said below
- w_qkv: float32 [2, 1024, 3, 1024], P(None, 'dp', None, 'tensor'), as said below
- w_out: float32 [2, 1024, 1024], P(None, 'dp', 'tensor'), may hold values from -0.75 to 0.75
- w_fc1: float32 [2, 1024, 4096], P(None, 'dp', 'tensor'), may hold values from -0.1875 to 0.1875
- w_fc2: float32 [2, 1024, 4096], P(None, 'dp', 'tensor'), may hold values from -0.09375 to 0.09375
- vec_small: float32 [2, 8, 1024], P(None, None, 'tensor'), as said below
- fc1_bias: float32 [2, 4096], P(None, 'tensor'), may hold values from -3 to 3
- mom_qkv: float32 [2, 2, 1024, 3, 1024], P(None, None, 'dp', None, 'tensor'), as said below
- mom_out: float32 [2, 2, 1024, 1024], P(None, None, 'dp', 'tensor'), as said below
- mom_fc1: float32 [2, 2, 1024, 4096], P(None, None, 'dp', 'tensor'), as said below
- mom_fc2: float32 [2, 2, 1024, 4096], P(None, None, 'dp', 'tensor'), as said below
- mom_vec: float32 [2, 2, 8, 1024], P(None, None, None, 'tensor'), as said below
- mom_bias: float32 [2, 2, 4096], P(None, None, 'tensor'), as said below
Outputs:
- output: float32 [16, 577, 1024], P('dp', None, 'tensor')
- input_grad: float32 [16, 577, 1024], P('dp', None, 'tensor')
- grad_qkv: float32 [2, 1024, 3, 1024], P(None, 'dp', None, 'tensor')
- grad_out: float32 [2, 1024, 1024], P(None, 'dp', 'tensor')
- grad_fc1: float32 [2, 1024, 4096], P(None, 'dp', 'tensor')
- grad_fc2: float32 [2, 1024, 4096], P(None, 'dp', 'tensor')
- grad_vec: float32 [2, 8, 1024], P(None, None, 'tensor')
- grad_bias: float32 [2, 4096], P(None, 'tensor')
- new_qkv: float32 [2, 1024, 3, 1024], P(None, 'dp', None, 'tensor')
- new_out: float32 [2, 1024, 1024], P(None, 'dp', 'tensor')
- new_fc1: float32 [2, 1024, 4096], P(None, 'dp', 'tensor')
- new_fc2: float32 [2, 1024, 4096], P(None, 'dp', 'tensor')
- new_vec: float32 [2, 8, 1024], P(None, None, 'tensor')
- new_bias: float32 [2, 4096], P(None, 'tensor')
- newmom_qkv: float32 [2, 2, 1024, 3, 1024], P(None, None, 'dp', None, 'tensor')
- newmom_out: float32 [2, 2, 1024, 1024], P(None, None, 'dp', 'tensor')
- newmom_fc1: float32 [2, 2, 1024, 4096], P(None, None, 'dp', 'tensor')
- newmom_fc2: float32 [2, 2, 1024, 4096], P(None, None, 'dp', 'tensor')
- newmom_vec: float32 [2, 2, 8, 1024], P(None, None, None, 'tensor')
- newmom_bias: float32 [2, 2, 4096], P(None, None, 'tensor')
Inputs may be any that keep to these rules, and one draw needn't show every extreme that they name: Every index of dp holds 1 or 2 images; some index holds 2 and some holds 1. Slot 2 i always holds an image, slot 2 i + 1 only where image_counts[i] is 2; other slots' tokens and cotangents are ignored. `w_qkv`: independent entries of mean 0 and deviation 1024^-0.5. `vec_small`: gains and shifts of order one. `mom_qkv`: second moments (index 1 of dimension 0) are positive. `mom_out`: second moments (index 1 of dimension 0) are positive. `mom_fc1`: second moments (index 1 of dimension 0) are positive. `mom_fc2`: second moments (index 1 of dimension 0) are positive. `mom_vec`: second moments (index 1 of dimension 0) are positive. `mom_bias`: second moments (index 1 of dimension 0) are positive.
All inputs are finite; a program needn't handle non-finite values.
Results may differ from a plain program's by a relative error of at most 0.022.
Values may be sent and summed in bfloat16 or wider, within the bound.
A program may use at most 256 MiB of HBM per device.

v0:
```python
import jax
import jax.numpy as jnp
from jax import lax
from jax.sharding import PartitionSpec as P

D = 1024
HEADS = 16
LAYERS = 2
STEP = 10
NORM_EPS = 1e-06
ROOT_HALF = 0.7071067811865476
INV_ROOT_TWO_PI = 0.3989422804014327
LEARN_RATE = 0.01
BETA_ONE = 0.9
BETA_TWO = 0.999
ADAM_EPS = 1e-08
WEIGHT_DECAY = 0.05
CONTRACT_LAST = (((1,), (1,)), ((), ()))
CONTRACT_FIRST = (((0,), (0,)), ((), ()))


def as_sent(shard):
    return jax.tree.map(lambda a: a.astype(jnp.bfloat16) if a.dtype == jnp.float32 else a, shard)


def gelu_value(preactivation):
    return 0.5 * preactivation * (1.0 + jax.scipy.special.erf(preactivation * ROOT_HALF))


def gelu_slope(preactivation):
    return (
        0.5 * (1.0 + jax.scipy.special.erf(preactivation * ROOT_HALF))
        + preactivation * jnp.exp(-0.5 * preactivation * preactivation) * INV_ROOT_TWO_PI
    )


def layer_statistics(hidden_state):
    totals = lax.psum(
        (jnp.sum(hidden_state, -1), jnp.sum(hidden_state * hidden_state, -1)), "tensor"
    )
    mean_row = totals[0][..., None] / D
    spread = totals[1][..., None] / D - mean_row * mean_row
    inv_std = lax.rsqrt(spread + NORM_EPS)
    return ((hidden_state - mean_row) * inv_std, inv_std)


def norm_back(d_normed, normed, inv_std, gain, carried):
    d_hat = d_normed * gain
    totals = lax.psum((jnp.sum(d_hat, -1), jnp.sum(d_hat * normed, -1)), "tensor")
    grad_in = carried + inv_std * (
        d_hat - totals[0][..., None] / D - normed * totals[1][..., None] / D
    )
    return (grad_in, jnp.sum(d_normed * normed, (0, 1)), jnp.sum(d_normed, (0, 1)))


def share_features(local_rows):
    return lax.all_gather(local_rows, "tensor", axis=2, tiled=True)


def sum_branch(partial_rows):
    return lax.psum_scatter(partial_rows, "tensor", scatter_dimension=2, tiled=True)


def share_grads(local_rows):
    return lax.all_gather(local_rows, "tensor", axis=2, tiled=True)


def sum_inputs(partial_rows):
    return lax.psum_scatter(
        partial_rows.astype(jnp.bfloat16), "tensor", scatter_dimension=2, tiled=True
    ).astype(jnp.float32)


def fetch_weights(w_qkv, w_out, w_fc1, w_fc2, layer_number):
    pieces = (
        w_qkv[layer_number].astype(jnp.bfloat16),
        w_out[layer_number].astype(jnp.bfloat16),
        w_fc1[layer_number].astype(jnp.bfloat16),
        w_fc2[layer_number].astype(jnp.bfloat16),
    )
    return (
        lax.all_gather(pieces[0], "dp", axis=0, tiled=True),
        lax.all_gather(pieces[1], "dp", axis=0, tiled=True),
        lax.all_gather(pieces[2], "dp", axis=0, tiled=True),
        lax.all_gather(pieces[3], "dp", axis=0, tiled=True),
    )


def attend_forward(query_h, key_h, value_h, attn_scale):
    scores = (
        jnp.einsum("bqhd,bkhd->bhqk", query_h, key_h, preferred_element_type=jnp.float32)
        * attn_scale
    )
    top_score = jnp.max(scores, -1, keepdims=True)
    logged_total = top_score + jnp.log(jnp.sum(jnp.exp(scores - top_score), -1, keepdims=True))
    probs = jnp.exp(scores - logged_total).astype(jnp.bfloat16)
    attention_result = jnp.einsum(
        "bhqk,bkhd->bqhd", probs, value_h, preferred_element_type=jnp.float32
    ).astype(jnp.bfloat16)
    return (attention_result, logged_total)


def attend_backward(query_h, key_h, value_h, attention_result, d_att, logged_total, attn_scale):
    scores = (
        jnp.einsum("bqhd,bkhd->bhqk", query_h, key_h, preferred_element_type=jnp.float32)
        * attn_scale
    )
    probs = jnp.exp(scores - logged_total)
    probs_low = probs.astype(jnp.bfloat16)
    d_value = jnp.einsum("bhqk,bqhd->bkhd", probs_low, d_att, preferred_element_type=jnp.float32)
    d_probs = jnp.einsum("bqhd,bkhd->bhqk", d_att, value_h, preferred_element_type=jnp.float32)
    delta = jnp.sum(d_att.astype(jnp.float32) * attention_result.astype(jnp.float32), -1)
    d_scores = (probs * (d_probs - jnp.swapaxes(delta, 1, 2)[..., None]) * attn_scale).astype(
        jnp.bfloat16
    )
    d_query = jnp.einsum("bhqk,bkhd->bqhd", d_scores, key_h, preferred_element_type=jnp.float32)
    d_key = jnp.einsum("bhqk,bqhd->bkhd", d_scores, query_h, preferred_element_type=jnp.float32)
    return (d_query, d_key, d_value)


def adam_update(param, running_gradient, moments, decay):
    first = BETA_ONE * moments[0] + (1.0 - BETA_ONE) * running_gradient
    second = BETA_TWO * moments[1] + (1.0 - BETA_TWO) * running_gradient * running_gradient
    fix_one = 1.0 - BETA_ONE**STEP
    fix_two = 1.0 - BETA_TWO**STEP
    update = first / fix_one / (jnp.sqrt(second / fix_two) + ADAM_EPS) + decay * param
    return (param - LEARN_RATE * update, jnp.stack([first, second]))


def on_device(
    tokens,
    cotangent,
    image_counts,
    w_qkv,
    w_out,
    w_fc1,
    w_fc2,
    vec_small,
    fc1_bias,
    mom_qkv,
    mom_out,
    mom_fc1,
    mom_fc2,
    mom_vec,
    mom_bias,
):
    slot_count, seq_len, feat_width = tokens.shape
    tok_rows = slot_count * seq_len
    heads_here = HEADS // lax.axis_size("tensor")
    head_dim = feat_width // heads_here
    attn_scale = head_dim ** (-0.5)
    slot_live = jnp.stack([jnp.ones((), jnp.float32), (image_counts[0] == 2).astype(jnp.float32)])[
        :, None, None
    ]

    def to_heads(matrix):
        return matrix.reshape(slot_count, seq_len, heads_here, head_dim)

    def to_slots(matrix):
        return matrix.reshape(slot_count, seq_len, -1)

    hidden_state = tokens.astype(jnp.float32)
    saved_tensors = []
    fetched = []
    for layer_number in range(LAYERS):
        weights = fetch_weights(w_qkv, w_out, w_fc1, w_fc2, layer_number)
        fetched.append(weights)
        projection_weight, backward_weight, first_weight, second_weight = weights
        vector_rows = vec_small[layer_number]
        first_centered_scaled, first_inverse_deviation = layer_statistics(hidden_state)
        first_normalized = share_features(
            (first_centered_scaled * vector_rows[0] + vector_rows[1]).astype(jnp.bfloat16)
        ).reshape(tok_rows, -1)
        proj_out = lax.dot_general(
            first_normalized,
            projection_weight,
            (((1,), (0,)), ((), ())),
            preferred_element_type=jnp.float32,
        )
        query_matrix_rows = (proj_out[:, 0] + vector_rows[2]).astype(jnp.bfloat16)
        key_matrix_rows = proj_out[:, 1].astype(jnp.bfloat16)
        value_matrix_rows = (proj_out[:, 2] + vector_rows[3]).astype(jnp.bfloat16)
        attention_result, logged_total = attend_forward(
            to_heads(query_matrix_rows),
            to_heads(key_matrix_rows),
            to_heads(value_matrix_rows),
            attn_scale,
        )
        attention_result = attention_result.reshape(tok_rows, feat_width)
        attn_branch = sum_branch(
            to_slots(
                lax.dot_general(
                    attention_result,
                    backward_weight,
                    CONTRACT_LAST,
                    preferred_element_type=jnp.float32,
                )
            )
        )
        middle_state = hidden_state + attn_branch + vector_rows[4]
        second_centered_scaled, second_inverse_deviation = layer_statistics(middle_state)
        second_normalized = share_features(
            (second_centered_scaled * vector_rows[5] + vector_rows[6]).astype(jnp.bfloat16)
        ).reshape(tok_rows, -1)
        preactivation = (
            jnp.dot(second_normalized, first_weight, preferred_element_type=jnp.float32)
            + fc1_bias[layer_number]
        )
        activation_narrow = gelu_value(preactivation).astype(jnp.bfloat16)
        branch_two = lax.dot_general(
            activation_narrow, second_weight, CONTRACT_LAST, preferred_element_type=jnp.float32
        )
        new_hidden = middle_state + sum_branch(to_slots(branch_two)) + vector_rows[7]
        saved_tensors.append(
            (
                first_centered_scaled,
                first_inverse_deviation,
                first_normalized,
                query_matrix_rows,
                key_matrix_rows,
                value_matrix_rows,
                attention_result,
                logged_total,
                second_centered_scaled,
                second_inverse_deviation,
                second_normalized,
                preactivation,
                activation_narrow,
            )
        )
        hidden_state = new_hidden
    output = hidden_state * slot_live
    running_gradient = cotangent * slot_live
    big_grads = [None] * LAYERS
    vec_grads = [None] * LAYERS
    bias_grads = [None] * LAYERS
    for layer_number in reversed(range(LAYERS)):
        projection_weight, backward_weight, first_weight, second_weight = fetch_weights(
            w_qkv, w_out, w_fc1, w_fc2, layer_number
        )
        vector_rows = vec_small[layer_number]
        (
            first_centered_scaled,
            first_inverse_deviation,
            first_normalized,
            query_matrix_rows,
            key_matrix_rows,
            value_matrix_rows,
            attention_result,
            logged_total,
            second_centered_scaled,
            second_inverse_deviation,
            second_normalized,
            preactivation,
            activation_narrow,
        ) = saved_tensors[layer_number]
        full_grad = share_grads(running_gradient.astype(jnp.bfloat16)).reshape(tok_rows, -1)
        g_fc2 = lax.dot_general(
            full_grad, activation_narrow, CONTRACT_FIRST, preferred_element_type=jnp.float32
        )
        g_bias_two = jnp.sum(running_gradient, (0, 1))
        d_pre = jnp.dot(full_grad, second_weight, preferred_element_type=jnp.float32) * gelu_slope(
            preactivation
        )
        d_pre_low = d_pre.astype(jnp.bfloat16)
        g_fc1 = lax.dot_general(
            second_normalized, d_pre_low, CONTRACT_FIRST, preferred_element_type=jnp.float32
        )
        g_fc1_bias = jnp.sum(d_pre, 0)
        second_normed_gradient = sum_inputs(
            to_slots(
                lax.dot_general(
                    d_pre_low, first_weight, CONTRACT_LAST, preferred_element_type=jnp.float32
                )
            )
        )
        middle_gradient, second_gain_gradient, second_shift_gradient = norm_back(
            second_normed_gradient,
            second_centered_scaled,
            second_inverse_deviation,
            vector_rows[5],
            running_gradient,
        )
        full_mid = share_grads(middle_gradient.astype(jnp.bfloat16)).reshape(tok_rows, -1)
        g_out = lax.dot_general(
            full_mid, attention_result, CONTRACT_FIRST, preferred_element_type=jnp.float32
        )
        g_bias_out = jnp.sum(middle_gradient, (0, 1))
        d_att = jnp.dot(full_mid, backward_weight, preferred_element_type=jnp.float32).astype(
            jnp.bfloat16
        )
        d_query, d_key, d_value = attend_backward(
            to_heads(query_matrix_rows),
            to_heads(key_matrix_rows),
            to_heads(value_matrix_rows),
            to_heads(attention_result),
            to_heads(d_att),
            logged_total,
            attn_scale,
        )
        d_query = d_query.reshape(tok_rows, feat_width)
        d_key = d_key.reshape(tok_rows, feat_width)
        d_value = d_value.reshape(tok_rows, feat_width)
        d_proj = jnp.stack([d_query, d_key, d_value], axis=1).astype(jnp.bfloat16)
        g_qkv = lax.dot_general(
            first_normalized, d_proj, CONTRACT_FIRST, preferred_element_type=jnp.float32
        )
        first_normed_gradient = sum_inputs(
            to_slots(
                lax.dot_general(
                    d_proj,
                    projection_weight,
                    (((1, 2), (1, 2)), ((), ())),
                    preferred_element_type=jnp.float32,
                )
            )
        )
        running_gradient, first_gain_gradient, first_shift_gradient = norm_back(
            first_normed_gradient,
            first_centered_scaled,
            first_inverse_deviation,
            vector_rows[0],
            middle_gradient,
        )
        vec_grads[layer_number] = jnp.stack(
            [
                first_gain_gradient,
                first_shift_gradient,
                jnp.sum(d_query, 0),
                jnp.sum(d_value, 0),
                g_bias_out,
                second_gain_gradient,
                second_shift_gradient,
                g_bias_two,
            ]
        )
        bias_grads[layer_number] = g_fc1_bias
        layer_tuple = (g_qkv, g_out, g_fc1, g_fc2)
        big_grads[layer_number] = layer_tuple
    input_grad = running_gradient * slot_live
    stacked = tuple((jnp.stack([entry[which] for entry in big_grads]) for which in range(4)))
    stacked = jax.tree.map(
        lambda part: part.astype(jnp.float32),
        lax.psum_scatter(as_sent(stacked), "dp", scatter_dimension=1, tiled=True),
    )
    small_sums = lax.psum((jnp.stack(vec_grads), jnp.stack(bias_grads)), "dp")
    grad_totals = (stacked[0], stacked[1], stacked[2], stacked[3], small_sums[0], small_sums[1])
    params = (w_qkv, w_out, w_fc1, w_fc2, vec_small, fc1_bias)
    moments = (mom_qkv, mom_out, mom_fc1, mom_fc2, mom_vec, mom_bias)
    decays = (WEIGHT_DECAY, WEIGHT_DECAY, WEIGHT_DECAY, WEIGHT_DECAY, 0.0, 0.0)
    results = [
        adam_update(param, grad_total, moment, decay)
        for param, grad_total, moment, decay in zip(params, grad_totals, moments, decays)
    ]
    return (
        output,
        input_grad,
        grad_totals[0],
        grad_totals[1],
        grad_totals[2],
        grad_totals[3],
        grad_totals[4],
        grad_totals[5],
        results[0][0],
        results[1][0],
        results[2][0],
        results[3][0],
        results[4][0],
        results[5][0],
        results[0][1],
        results[1][1],
        results[2][1],
        results[3][1],
        results[4][1],
        results[5][1],
    )


def solution(mesh):
    return jax.shard_map(
        on_device,
        mesh=mesh,
        in_specs=(
            P("dp", None, "tensor"),
            P("dp", None, "tensor"),
            P("dp"),
            P(None, "dp", None, "tensor"),
            P(None, "dp", "tensor"),
            P(None, "dp", "tensor"),
            P(None, "dp", "tensor"),
            P(None, None, "tensor"),
            P(None, "tensor"),
            P(None, None, "dp", None, "tensor"),
            P(None, None, "dp", "tensor"),
            P(None, None, "dp", "tensor"),
            P(None, None, "dp", "tensor"),
            P(None, None, None, "tensor"),
            P(None, None, "tensor"),
        ),
        out_specs=(
            P("dp", None, "tensor"),
            P("dp", None, "tensor"),
            P(None, "dp", None, "tensor"),
            P(None, "dp", "tensor"),
            P(None, "dp", "tensor"),
            P(None, "dp", "tensor"),
            P(None, None, "tensor"),
            P(None, "tensor"),
            P(None, "dp", None, "tensor"),
            P(None, "dp", "tensor"),
            P(None, "dp", "tensor"),
            P(None, "dp", "tensor"),
            P(None, None, "tensor"),
            P(None, "tensor"),
            P(None, None, "dp", None, "tensor"),
            P(None, None, "dp", "tensor"),
            P(None, None, "dp", "tensor"),
            P(None, None, "dp", "tensor"),
            P(None, None, None, "tensor"),
            P(None, None, "tensor"),
        ),
        check_vma=False,
    )
```

profile of v0, /device:TPU:0, one launch (start us, length us, event | category | flops | bytes accessed | tf_op | source)
XLA Modules:
  0.0 1669.3 jit_solution(3100951194035109462)
XLA Ops:
  9.8 20.6 %all-reduce.8 = (f32[2,577]{1,0:T(2,128)S(1)}, f32[2,577]{1,0:T(2,128)S(1)}) all-reduce(f32[2,577]{1,0:T(2,128)S(1)} %get-tuple-element.103, f32[2,577]{1,0:T(2,128)S(1)} %get-tuple-element.102), channel_id=1, replica_groups=mesh['dp'=8,'tensor'=4] {'tensor'}, use_global_device_ids=true, to_apply=%region_3.0 | all-reduce | flops 2308 | bytes 18464 | tf_op jit(solution)/shard_map/psum | solution.py:38
  33.9 9.9 all-gather.1
  43.8 38.4 %all-gather.23.cloned.1.call-done = bf16[2,577,1024]{2,1,0:T(8,128)(2,1)} async-done(((bf16[2,577,256]{2,1,0:T(8,128)(2,1)}), bf16[2,577,1024]{2,1,0:T(8,128)(2,1)}) %all-gather.23.cloned.1.call-update) | async-done | bytes 2363408 | tf_op jit(solution)/shard_map/all_gather | solution.py:57
  85.7 22.7 %all-gather.39.cloned.1.call-done = bf16[1,1024,3,256]{3,1,2,0:T(8,128)(2,1)} async-done(((bf16[1,128,3,256]{3,1,2,0:T(8,128)(2,1)}), bf16[1,1024,3,256]{3,1,2,0:T(8,128)(2,1)}) %all-gather.39.cloned.1.call-update) | async-done | bytes 1572880 | tf_op jit(solution)/shard_map/all_gather | solution.py:82
  142.3 86.5 %reduce-scatter.13.cloned.1.call-done = f32[2,577,256]{2,1,0:T(8,128)} async-done(((f32[2,577,1024]{2,1,0:T(8,128)}), f32[2,577,256]{2,1,0:T(8,128)}) %reduce-scatter.13.cloned.1.call-update) | async-done | bytes 1181712 | tf_op jit(solution)/shard_map/reduce_scatter | solution.py:61
  230.6 17.9 %all-reduce.7 = (f32[2,577]{1,0:T(2,128)S(1)}, f32[2,577]{1,0:T(2,128)S(1)}) all-reduce(f32[2,577]{1,0:T(2,128)S(1)} %get-tuple-element.93, f32[2,577]{1,0:T(2,128)S(1)} %get-tuple-element.92), channel_id=1, replica_groups=mesh['dp'=8,'tensor'=4] {'tensor'}, use_global_device_ids=true, to_apply=%region_10.0 | all-reduce | flops 2308 | bytes 18464 | tf_op jit(solution)/shard_map/psum | solution.py:38
  253.2 46.1 %all-gather.25.cloned.1.call-done = bf16[2,577,1024]{2,1,0:T(8,128)(2,1)} async-done(((bf16[2,577,256]{2,1,0:T(8,128)(2,1)}), bf16[2,577,1024]{2,1,0:T(8,128)(2,1)}) %all-gather.25.cloned.1.call-update) | async-done | bytes 2363408 | tf_op jit(solution)/shard_map/all_gather | solution.py:57
  302.9 24.7 %all-gather.41.cloned.1.call-done = bf16[1,1024,1024]{2,1,0:T(8,128)(2,1)} async-done(((bf16[1,128,1024]{2,1,0:T(8,128)(2,1)}), bf16[1,1024,1024]{2,1,0:T(8,128)(2,1)}) %all-gather.41.cloned.1.call-update) | async-done | bytes 2097168 | tf_op jit(solution)/shard_map/all_gather | solution.py:84
  327.7 7.1 multiply_convert_fusion.3
  334.8 23.0 %all-gather.43.cloned.1.call-done = bf16[1,1024,1024]{2,1,0:T(8,128)(2,1)} async-done(((bf16[1,128,1024]{2,1,0:T(8,128)(2,1)}), bf16[1,1024,1024]{2,1,0:T(8,128)(2,1)}) %all-gather.43.cloned.1.call-update) | async-done | bytes 2097168 | tf_op jit(solution)/shard_map/all_gather | solution.py:85
  357.8 7.1 fusion.16
  369.9 86.5 %reduce-scatter.15.cloned.1.call-done = f32[2,577,256]{2,1,0:T(8,128)} async-done(((f32[2,577,1024]{2,1,0:T(8,128)}), f32[2,577,256]{2,1,0:T(8,128)}) %reduce-scatter.15.cloned.1.call-update) | async-done | bytes 1181712 | tf_op jit(solution)/shard_map/reduce_scatter | solution.py:61
  458.1 17.9 %all-reduce.6 = (f32[2,577]{1,0:T(2,128)S(1)}, f32[2,577]{1,0:T(2,128)S(1)}) all-reduce(f32[2,577]{1,0:T(2,128)S(1)} %get-tuple-element.91, f32[2,577]{1,0:T(2,128)S(1)} %get-tuple-element.90), channel_id=1, replica_groups=mesh['dp'=8,'tensor'=4] {'tensor'}, use_global_device_ids=true, to_apply=%region_15.0 | all-reduce | flops 2308 | bytes 18464 | tf_op jit(solution)/shard_map/psum | solution.py:38
  478.2 11.1 all-gather.5
  489.3 37.6 %all-gather.27.cloned.1.call-done = bf16[2,577,1024]{2,1,0:T(8,128)(2,1)} async-done(((bf16[2,577,256]{2,1,0:T(8,128)(2,1)}), bf16[2,577,1024]{2,1,0:T(8,128)(2,1)}) %all-gather.27.cloned.1.call-update) | async-done | bytes 2363408 | tf_op jit(solution)/shard_map/all_gather | solution.py:57
  530.4 22.7 %all-gather.45.cloned.1.call-done = bf16[1,1024,3,256]{3,1,2,0:T(8,128)(2,1)} async-done(((bf16[1,128,3,256]{3,1,2,0:T(8,128)(2,1)}), bf16[1,1024,3,256]{3,1,2,0:T(8,128)(2,1)}) %all-gather.45.cloned.1.call-update) | async-done | bytes 1572880 | tf_op jit(solution)/shard_map/all_gather | solution.py:82
  591.3 83.4 %reduce-scatter.17.cloned.1.call-done = f32[2,577,256]{2,1,0:T(8,128)} async-done(((f32[2,577,1024]{2,1,0:T(8,128)}), f32[2,577,256]{2,1,0:T(8,128)}) %reduce-scatter.17.cloned.1.call-update) | async-done | bytes 1181712 | tf_op jit(solution)/shard_map/reduce_scatter | solution.py:61
  677.1 18.6 %all-reduce.5 = (f32[2,577]{1,0:T(2,128)S(1)}, f32[2,577]{1,0:T(2,128)S(1)}) all-reduce(f32[2,577]{1,0:T(2,128)S(1)} %get-tuple-element.89, f32[2,577]{1,0:T(2,128)S(1)} %get-tuple-element.88), channel_id=1, replica_groups=mesh['dp'=8,'tensor'=4] {'tensor'}, use_global_device_ids=true, to_apply=%region_22.0 | all-reduce | flops 2308 | bytes 18464 | tf_op jit(solution)/shard_map/psum | solution.py:38
  700.1 28.4 %all-gather.31.cloned.1.call-done = bf16[2,577,1024]{2,1,0:T(8,128)(2,1)} async-done(((bf16[2,577,256]{2,1,0:T(8,128)(2,1)}), bf16[2,577,1024]{2,1,0:T(8,128)(2,1)}) %all-gather.31.cloned.1.call-update) | async-done | bytes 2363408 | tf_op jit(solution)/shard_map/all_gather | solution.py:65
  732.0 47.8 %all-gather.29.cloned.1.call-done = bf16[2,577,1024]{2,1,0:T(8,128)(2,1)} async-done(((bf16[2,577,256]{2,1,0:T(8,128)(2,1)}), bf16[2,577,1024]{2,1,0:T(8,128)(2,1)}) %all-gather.29.cloned.1.call-update) | async-done | bytes 2363408 | tf_op jit(solution)/shard_map/all_gather | solution.py:57
  783.4 24.9 %all-gather.47.cloned.1.call-done = bf16[1,1024,1024]{2,1,0:T(8,128)(2,1)} async-done(((bf16[1,128,1024]{2,1,0:T(8,128)(2,1)}), bf16[1,1024,1024]{2,1,0:T(8,128)(2,1)}) %all-gather.47.cloned.1.call-update) | async-done | bytes 2097168 | tf_op jit(solution)/shard_map/all_gather | solution.py:84
  808.3 7.2 multiply_convert_fusion.2
  815.5 22.9 %all-gather.49.cloned.1.call-done = bf16[1,1024,1024]{2,1,0:T(8,128)(2,1)} async-done(((bf16[1,128,1024]{2,1,0:T(8,128)(2,1)}), bf16[1,1024,1024]{2,1,0:T(8,128)(2,1)}) %all-gather.49.cloned.1.call-update) | async-done | bytes 2097168 | tf_op jit(solution)/shard_map/all_gather | solution.py:85
  838.4 7.1 fusion.135
  854.6 7.2 fusion.11
  861.8 5.0 reshape.286
  866.8 36.1 %reduce-scatter.21.cloned.1.call-done = bf16[2,577,256]{2,1,0:T(8,128)(2,1)} async-done(((bf16[2,577,1024]{2,1,0:T(8,128)(2,1)}), bf16[2,577,256]{2,1,0:T(8,128)(2,1)}) %reduce-scatter.21.cloned.1.call-update) | async-done | bytes 590864 | tf_op jit(solution)/shard_map/reduce_scatter | solution.py:69
  905.2 18.0 %all-reduce.4 = (f32[2,577]{1,0:T(2,128)S(1)}, f32[2,577]{1,0:T(2,128)S(1)}) all-reduce(f32[2,577]{1,0:T(2,128)S(1)} %get-tuple-element.83, f32[2,577]{1,0:T(2,128)S(1)} %get-tuple-element.96), channel_id=1, replica_groups=mesh['dp'=8,'tensor'=4] {'tensor'}, use_global_device_ids=true, to_apply=%region_28.0 | all-reduce | flops 2308 | bytes 18464 | tf_op jit(solution)/shard_map/psum | solution.py:49
  923.2 68.0 %reduce-scatter.19.cloned.1.call-done = f32[2,577,256]{2,1,0:T(8,128)} async-done(((f32[2,577,1024]{2,1,0:T(8,128)}), f32[2,577,256]{2,1,0:T(8,128)}) %reduce-scatter.19.cloned.1.call-update) | async-done | bytes 1181712 | tf_op jit(solution)/shard_map/reduce_scatter | solution.py:61
  996.7 51.5 %all-gather.33.cloned.1.call-done = bf16[2,577,1024]{2,1,0:T(8,128)(2,1)} async-done(((bf16[2,577,256]{2,1,0:T(8,128)(2,1)}), bf16[2,577,1024]{2,1,0:T(8,128)(2,1)}) %all-gather.33.cloned.1.call-update) | async-done | bytes 2363408 | tf_op jit(solution)/shard_map/all_gather | solution.py:65
  1061.9 8.6 multiply_convert_fusion.1
  1109.2 46.6 %reduce-scatter.23.cloned.1.call-done = bf16[2,577,256]{2,1,0:T(8,128)(2,1)} async-done(((bf16[2,577,1024]{2,1,0:T(8,128)(2,1)}), bf16[2,577,256]{2,1,0:T(8,128)(2,1)}) %reduce-scatter.23.cloned.1.call-update) | async-done | bytes 590864 | tf_op jit(solution)/shard_map/reduce_scatter | solution.py:69
  1157.6 17.3 %all-reduce.3 = (f32[2,577]{1,0:T(2,128)S(1)}, f32[2,577]{1,0:T(2,128)S(1)}) all-reduce(f32[2,577]{1,0:T(2,128)S(1)} %get-tuple-element.85, f32[2,577]{1,0:T(2,128)S(1)} %get-tuple-element.95), channel_id=1, replica_groups=mesh['dp'=8,'tensor'=4] {'tensor'}, use_global_device_ids=true, to_apply=%region_34.0 | all-reduce | flops 2308 | bytes 18464 | tf_op jit(solution)/shard_map/psum | solution.py:49
  1179.3 49.1 %all-gather.35.cloned.1.call-done = bf16[2,577,1024]{2,1,0:T(8,128)(2,1)} async-done(((bf16[2,577,256]{2,1,0:T(8,128)(2,1)}), bf16[2,577,1024]{2,1,0:T(8,128)(2,1)}) %all-gather.35.cloned.1.call-update) | async-done | bytes 2363408 | tf_op jit(solution)/shard_map/all_gather | solution.py:65
  1232.0 7.1 fusion.136
  1248.1 46.6 %reduce-scatter.25.cloned.1.call-done = bf16[2,577,256]{2,1,0:T(8,128)(2,1)} async-done(((bf16[2,577,1024]{2,1,0:T(8,128)(2,1)}), bf16[2,577,256]{2,1,0:T(8,128)(2,1)}) %reduce-scatter.25.cloned.1.call-update) | async-done | bytes 590864 | tf_op jit(solution)/shard_map/reduce_scatter | solution.py:69
  1297.1 17.3 %all-reduce.2 = (f32[2,577]{1,0:T(2,128)S(1)}, f32[2,577]{1,0:T(2,128)S(1)}) all-reduce(f32[2,577]{1,0:T(2,128)S(1)} %get-tuple-element.81, f32[2,577]{1,0:T(2,128)S(1)} %get-tuple-element.97), channel_id=1, replica_groups=mesh['dp'=8,'tensor'=4] {'tensor'}, use_global_device_ids=true, to_apply=%region_39.0 | all-reduce | flops 2308 | bytes 18464 | tf_op jit(solution)/shard_map/psum | solution.py:49
  1319.1 5.5 convert_bitcast_fusion.2
  1330.4 5.5 convert_bitcast_fusion
  1352.9 14.9 all-gather.37.cloned.1.call-done
  1380.3 6.8 multiply_convert_fusion
  1389.7 7.4 fusion.125
  1432.5 42.5 %reduce-scatter.35.cloned.1.call-done = bf16[2,128,1024]{2,1,0:T(8,128)(2,1)} async-done(((bf16[2,1024,1024]{2,1,0:T(8,128)(2,1)}), bf16[2,128,1024]{2,1,0:T(8,128)(2,1)}) %reduce-scatter.35.cloned.1.call-update) | async-done | bytes 524304 | tf_op jit(solution)/shard_map/reduce_scatter | solution.py:344
  1479.8 34.9 %reduce-scatter.31.cloned.1.call-done = bf16[2,128,256]{2,1,0:T(8,128)(2,1)} async-done(((bf16[2,1024,256]{2,1,0:T(8,128)(2,1)}), bf16[2,128,256]{2,1,0:T(8,128)(2,1)}) %reduce-scatter.31.cloned.1.call-update) | async-done | bytes 131088 | tf_op jit(solution)/shard_map/reduce_scatter | solution.py:344
  1517.4 46.7 %reduce-scatter.29.cloned.1.call-done = bf16[2,128,3,256]{3,1,2,0:T(8,128)(2,1)} async-done(((bf16[2,1024,3,256]{3,1,2,0:T(8,128)(2,1)}), bf16[2,128,3,256]{3,1,2,0:T(8,128)(2,1)}) %reduce-scatter.29.cloned.1.call-update) | async-done | bytes 393232 | tf_op jit(solution)/shard_map/reduce_scatter | solution.py:344
  1568.1 46.5 %reduce-scatter.27.cloned.1.call-done = bf16[2,577,256]{2,1,0:T(8,128)(2,1)} async-done(((bf16[2,577,1024]{2,1,0:T(8,128)(2,1)}), bf16[2,577,256]{2,1,0:T(8,128)(2,1)}) %reduce-scatter.27.cloned.1.call-update) | async-done | bytes 590864 | tf_op jit(solution)/shard_map/reduce_scatter | solution.py:69
  1616.5 17.3 %all-reduce.1 = (f32[2,577]{1,0:T(2,128)S(1)}, f32[2,577]{1,0:T(2,128)S(1)}) all-reduce(f32[2,577]{1,0:T(2,128)S(1)} %get-tuple-element.87, f32[2,577]{1,0:T(2,128)S(1)} %get-tuple-element.94), channel_id=1, replica_groups=mesh['dp'=8,'tensor'=4] {'tensor'}, use_global_device_ids=true, to_apply=%region_45.0 | all-reduce | flops 2308 | bytes 18464 | tf_op jit(solution)/shard_map/psum | solution.py:49
  1637.3 22.4 %all-reduce = (f32[2,8,256]{2,1,0:T(8,128)S(1)}, f32[2,1024]{1,0:T(2,128)S(1)}) all-reduce(f32[2,8,256]{2,1,0:T(8,128)S(1)} %pad_maximum_fusion.9, f32[2,1024]{1,0:T(2,128)S(1)} %pad_maximum_fusion.11), channel_id=1, replica_groups=mesh['dp'=8,'tensor'=4] {'dp'}, use_global_device_ids=true, to_apply=%region_66.0 | all-reduce | flops 6144 | bytes 49152 | tf_op jit(solution)/shard_map/psum | solution.py:346
  (381 shorter events, 303.9 us)
Async XLA Ops:
  7.2 25.6 %copy-start.30 = (f32[2,128,3,256]{3,1,2,0:T(8,128)S(1)}, f32[2,128,3,256]{3,1,2,0:T(8,128)}, u32[]{:S(2)}) copy-start(f32[2,128,3,256]{3,1,2,0:T(8,128)} %param.18) | copy-start | bytes 2359300
  7.2 75.0 %all-gather.23.cloned.1.call-start = ((), (), s32[]{:S(2)}) async-start(), calls=%async_computation.12 | async-start | bytes 2990080 | tf_op jit(solution)/shard_map/all_gather | solution.py:57
  8.3 24.4 %copy-start.65 = (f32[1,1,256]{2,1,0:T(1,128)}, f32[1,1,256]{2,1,0:T(1,128)S(1)}, u32[]{:S(2)}) copy-start(f32[1,1,256]{2,1,0:T(1,128)S(1)} %get-tuple-element.194) | copy-start | bytes 3076
  32.7 75.7 %all-gather.39.cloned.1.call-start = ((), (), s32[]{:S(2)}) async-start(), calls=%async_computation.32 | async-start | bytes 1769472 | tf_op jit(solution)/shard_map/all_gather | solution.py:82
  33.6 195.1 %reduce-scatter.13.cloned.1.call-start = ((), (), s32[]{:S(2)}) async-start(), calls=%async_computation.13 | async-start | bytes 5980160 | tf_op jit(solution)/shard_map/reduce_scatter | solution.py:61
  33.8 94.7 %copy-start.56 = (f32[4,64]{1,0:T(4,128)}, f32[4,64]{1,0:T(4,128)S(1)}, u32[]{:S(2)}) copy-start(f32[4,64]{1,0:T(4,128)S(1)} %add.365) | copy-start | bytes 3076
  33.9 100.7 %copy-start.58 = (f32[4,64]{1,0:T(4,128)}, f32[4,64]{1,0:T(4,128)S(1)}, u32[]{:S(2)}) copy-start(f32[4,64]{1,0:T(4,128)S(1)} %add.362) | copy-start | bytes 3076
  43.8 95.4 %copy-start.37 = (bf16[1,1024,256]{2,1,0:T(8,128)(2,1)}, bf16[1,1024,256]{2,1,0:T(8,128)(2,1)S(1)}, u32[]{:S(2)}) copy-start(bf16[1,1024,256]{2,1,0:T(8,128)(2,1)S(1)} %all-gather.1) | copy-start | bytes 1572868
  142.2 86.5 %copy-start.5 = (bf16[2,577,256]{2,0,1:T(2,128)(2,1)S(1)}, bf16[2,577,256]{2,0,1:T(2,128)(2,1)}, u32[]{:S(2)}) copy-start(bf16[2,577,256]{2,0,1:T(2,128)(2,1)} %param.15) | copy-start | bytes 1772548
  142.3 157.1 %all-gather.25.cloned.1.call-start = ((), (), s32[]{:S(2)}) async-start(), calls=%async_computation.14 | async-start | bytes 2990080 | tf_op jit(solution)/shard_map/all_gather | solution.py:57
  249.8 77.9 %all-gather.41.cloned.1.call-start = ((), (), s32[]{:S(2)}) async-start(), calls=%async_computation.33 | async-start | bytes 2359296 | tf_op jit(solution)/shard_map/all_gather | solution.py:84
  250.8 107.0 %all-gather.43.cloned.1.call-start = ((), (), s32[]{:S(2)}) async-start(), calls=%async_computation.34 | async-start | bytes 2359296 | tf_op jit(solution)/shard_map/all_gather | solution.py:85
  253.0 203.4 %reduce-scatter.15.cloned.1.call-start = ((), (), s32[]{:S(2)}) async-start(), calls=%async_computation.15 | async-start | bytes 5980160 | tf_op jit(solution)/shard_map/reduce_scatter | solution.py:61
  369.9 157.0 %all-gather.27.cloned.1.call-start = ((), (), s32[]{:S(2)}) async-start(), calls=%async_computation.16 | async-start | bytes 2990080 | tf_op jit(solution)/shard_map/all_gather | solution.py:57
  477.3 75.9 %all-gather.45.cloned.1.call-start = ((), (), s32[]{:S(2)}) async-start(), calls=%async_computation.35 | async-start | bytes 1769472 | tf_op jit(solution)/shard_map/all_gather | solution.py:82
  478.0 196.7 %reduce-scatter.17.cloned.1.call-start = ((), (), s32[]{:S(2)}) async-start(), calls=%async_computation.17 | async-start | bytes 5980160 | tf_op jit(solution)/shard_map/reduce_scatter | solution.py:61
  588.2 140.3 %all-gather.31.cloned.1.call-start = ((), (), s32[]{:S(2)}) async-start(), calls=%async_computation.20 | async-start | bytes 2990080 | tf_op jit(solution)/shard_map/all_gather | solution.py:65
  588.9 402.3 %copy-start.68 = (f32[2]{0:T(128)}, f32[2]{0:T(128)S(1)}, u32[]{:S(2)}) copy-start(f32[2]{0:T(128)S(1)} %add_convert_fusion.15) | copy-start | bytes 28
  591.2 188.6 %all-gather.29.cloned.1.call-start = ((), (), s32[]{:S(2)}) async-start(), calls=%async_computation.18 | async-start | bytes 2990080 | tf_op jit(solution)/shard_map/all_gather | solution.py:57
  698.3 110.0 %all-gather.47.cloned.1.call-start = ((), (), s32[]{:S(2)}) async-start(), calls=%async_computation.36 | async-start | bytes 2359296 | tf_op jit(solution)/shard_map/all_gather | solution.py:84
  699.0 139.4 %all-gather.49.cloned.1.call-start = ((), (), s32[]{:S(2)}) async-start(), calls=%async_computation.37 | async-start | bytes 2359296 | tf_op jit(solution)/shard_map/all_gather | solution.py:85
  699.6 203.3 %reduce-scatter.21.cloned.1.call-start = ((), (), s32[]{:S(2)}) async-start(), calls=%async_computation.21 | async-start | bytes 2990080 | tf_op jit(solution)/shard_map/reduce_scatter | solution.py:69
  854.5 136.7 %reduce-scatter.19.cloned.1.call-start = ((), (), s32[]{:S(2)}) async-start(), calls=%async_computation.19 | async-start | bytes 5980160 | tf_op jit(solution)/shard_map/reduce_scatter | solution.py:61
  866.8 181.4 %all-gather.33.cloned.1.call-start = ((), (), s32[]{:S(2)}) async-start(), calls=%async_computation.22 | async-start | bytes 2990080 | tf_op jit(solution)/shard_map/all_gather | solution.py:65
  996.6 159.1 %reduce-scatter.23.cloned.1.call-start = ((), (), s32[]{:S(2)}) async-start(), calls=%async_computation.23 | async-start | bytes 2990080 | tf_op jit(solution)/shard_map/reduce_scatter | solution.py:69
  1109.2 119.3 %all-gather.35.cloned.1.call-start = ((), (), s32[]{:S(2)}) async-start(), calls=%async_computation.24 | async-start | bytes 2990080 | tf_op jit(solution)/shard_map/all_gather | solution.py:65
  1179.3 115.4 %reduce-scatter.25.cloned.1.call-start = ((), (), s32[]{:S(2)}) async-start(), calls=%async_computation.25 | async-start | bytes 2990080 | tf_op jit(solution)/shard_map/reduce_scatter | solution.py:69
  1248.0 66.3 %copy-start.16 = (f32[2,577,256]{2,1,0:T(8,128)S(1)}, f32[2,577,256]{2,1,0:T(8,128)}, u32[]{:S(2)}) copy-start(f32[2,577,256]{2,1,0:T(8,128)} %copy-done.15) | copy-start | bytes 3545092
  1248.1 119.7 %all-gather.37.cloned.1.call-start = ((), (), s32[]{:S(2)}) async-start(), calls=%async_computation.26 | async-start | bytes 2990080 | tf_op jit(solution)/shard_map/all_gather | solution.py:65
  1318.7 107.7 %reduce-scatter.33.cloned.1.call-start = ((), (), s32[]{:S(2)}) async-start(), calls=%async_computation.30 | async-start | bytes 4718592 | tf_op jit(solution)/shard_map/reduce_scatter | solution.py:344
  1330.3 144.7 %reduce-scatter.35.cloned.1.call-start = ((), (), s32[]{:S(2)}) async-start(), calls=%async_computation.31 | async-start | bytes 4718592 | tf_op jit(solution)/shard_map/reduce_scatter | solution.py:344
  1341.6 173.1 %reduce-scatter.31.cloned.1.call-start = ((), (), s32[]{:S(2)}) async-start(), calls=%async_computation.29 | async-start | bytes 1179648 | tf_op jit(solution)/shard_map/reduce_scatter | solution.py:344
  1397.2 166.9 %reduce-scatter.29.cloned.1.call-start = ((), (), s32[]{:S(2)}) async-start(), calls=%async_computation.28 | async-start | bytes 3538944 | tf_op jit(solution)/shard_map/reduce_scatter | solution.py:344
  1413.3 201.3 %reduce-scatter.27.cloned.1.call-start = ((), (), s32[]{:S(2)}) async-start(), calls=%async_computation.27 | async-start | bytes 2990080 | tf_op jit(solution)/shard_map/reduce_scatter | solution.py:69
  1431.1 43.9 %copy-start.24 = (f32[2,2,128,1024]{3,2,1,0:T(8,128)S(1)}, f32[2,2,128,1024]{3,2,1,0:T(8,128)}, u32[]{:S(2)}) copy-start(f32[2,2,128,1024]{3,2,1,0:T(8,128)} %param.27) | copy-start | bytes 6291460
  1478.2 36.5 %copy-start.41 = (f32[2,2,128,256]{3,2,1,0:T(8,128)S(1)}, f32[2,2,128,256]{3,2,1,0:T(8,128)}, u32[]{:S(2)}) copy-start(f32[2,2,128,256]{3,2,1,0:T(8,128)} %param.25) | copy-start | bytes 1572868
  1478.2 37.4 %copy-start.44 = (f32[2,128,256]{2,1,0:T(8,128)S(1)}, f32[2,128,256]{2,1,0:T(8,128)}, u32[]{:S(2)}) copy-start(f32[2,128,256]{2,1,0:T(8,128)} %param.19) | copy-start | bytes 786436
  1479.6 84.5 %copy-start.29 = (f32[2,2,128,3,256]{4,2,3,1,0:T(8,128)S(1)}, f32[2,2,128,3,256]{4,2,3,1,0:T(8,128)}, u32[]{:S(2)}) copy-start(f32[2,2,128,3,256]{4,2,3,1,0:T(8,128)} %param.24) | copy-start | bytes 4718596
  1515.6 49.6 %copy-start.42 = (f32[2,128,256]{2,1,0:T(8,128)}, f32[2,128,256]{2,1,0:T(8,128)S(1)}, u32[]{:S(2)}) copy-start(f32[2,128,256]{2,1,0:T(8,128)S(1)} %get-tuple-element.131) | copy-start | bytes 786436
  1516.5 48.7 %copy-start.31 = (f32[2,128,3,256]{3,1,2,0:T(8,128)S(1)}, f32[2,128,3,256]{3,1,2,0:T(8,128)}, u32[]{:S(2)}) copy-start(f32[2,128,3,256]{3,1,2,0:T(8,128)} %param.18) | copy-start | bytes 2359300
  1566.8 47.8 %copy-start.6 = (bf16[2,577,256]{2,0,1:T(2,128)(2,1)S(1)}, bf16[2,577,256]{2,0,1:T(2,128)(2,1)}, u32[]{:S(2)}) copy-start(bf16[2,577,256]{2,0,1:T(2,128)(2,1)} %param.15) | copy-start | bytes 1772548
  1566.8 47.8 %copy-start.52 = (f32[2,577]{1,0:T(2,128)S(1)}, f32[2,577]{1,0:T(2,128)}, u32[]{:S(2)}) copy-start(f32[2,577]{1,0:T(2,128)} %copy-done.51) | copy-start | bytes 13852
  1566.8 47.8 %copy-start.54 = (f32[2,577]{1,0:T(2,128)S(1)}, f32[2,577]{1,0:T(2,128)}, u32[]{:S(2)}) copy-start(f32[2,577]{1,0:T(2,128)} %copy-done.53) | copy-start | bytes 13852
  1566.8 47.8 %copy-start.66 = (f32[1,1,256]{2,1,0:T(1,128)S(1)}, f32[1,1,256]{2,1,0:T(1,128)}, u32[]{:S(2)}) copy-start(f32[1,1,256]{2,1,0:T(1,128)} %copy-done.65) | copy-start | bytes 3076
  1566.8 67.0 %copy-start.14 = (f32[2,577,256]{2,1,0:T(8,128)S(1)}, f32[2,577,256]{2,1,0:T(8,128)}, u32[]{:S(2)}) copy-start(f32[2,577,256]{2,1,0:T(8,128)} %copy-done.13) | copy-start | bytes 3545092
  1566.8 67.0 %copy-start.69 = (f32[2]{0:T(128)S(1)}, f32[2]{0:T(128)}, u32[]{:S(2)}) copy-start(f32[2]{0:T(128)} %copy-done.68) | copy-start | bytes 28
  1635.6 24.8 %copy-start.62 = (f32[2,1024]{1,0:T(2,128)S(1)}, f32[2,1024]{1,0:T(2,128)}, u32[]{:S(2)}) copy-start(f32[2,1024]{1,0:T(2,128)} %param.23) | copy-start | bytes 24580
  1635.7 24.7 %copy-start.63 = (f32[2,2,1024]{2,1,0:T(2,128)S(1)}, f32[2,2,1024]{2,1,0:T(2,128)}, u32[]{:S(2)}) copy-start(f32[2,2,1024]{2,1,0:T(2,128)} %param.29) | copy-start | bytes 49156
  (62 other events, 338.7 us)
Sparse Core Ops, SparseCore 0:
  32.8 49.2 all-gather.22
  84.6 23.7 all-gather.38
  142.4 86.3 reduce-scatter.12
  249.9 49.3 all-gather.24
  301.7 25.9 all-gather.40
  330.0 27.7 all-gather.42
  370.0 86.3 reduce-scatter.14
  477.4 49.4 all-gather.26
  529.4 23.7 all-gather.44
  588.3 86.3 reduce-scatter.16
  676.8 51.6 all-gather.30
  730.5 49.3 all-gather.28
  782.3 25.9 all-gather.46
  810.6 27.7 all-gather.48
  854.6 48.2 reduce-scatter.20
  905.1 86.0 reduce-scatter.18
  996.8 51.4 all-gather.32
  1109.3 46.4 reduce-scatter.22
  1179.4 48.9 all-gather.34
  1248.2 46.4 reduce-scatter.24
  1318.8 48.9 all-gather.36
  1371.2 49.2 reduce-scatter.32
  1423.8 51.1 reduce-scatter.34
  1478.6 35.9 reduce-scatter.30
  1518.0 46.0 reduce-scatter.28
  1566.3 48.2 reduce-scatter.26
where the time goes:
time: 1680 us; the launch traced here: 1670 us
  waiting for transfers between devices  1080 us (64%)
  blocking collectives  188 us (11%)
  matrix products  160 us (10%)
  local copies, waits for them, and re-layouts  148 us (9%)
  other arithmetic  72.7 us (4%)
    reduce_scatter x4, waiting for transfers between devices, sum_branch(): lax.psum_scatter(partial_rows, 'tensor', scatter_dimension=2, tiled=True)  324 us
    reduce_scatter x4, waiting for transfers between devices, sum_inputs(): lax.psum_scatter(partial_rows.astype(jnp.bfloat16), 'tensor', scatter_dim...  176 us
    all_gather x4, waiting for transfers between devices, share_features(): return lax.all_gather(local_rows, 'tensor', axis=2, tiled=True)  170 us
    all_gather x4, waiting for transfers between devices, share_grads(): return lax.all_gather(local_rows, 'tensor', axis=2, tiled=True)  144 us
    reduce_scatter x4, waiting for transfers between devices, on_device(): lax.psum_scatter(as_sent(stacked), 'dp', scatter_dimension=1, tiled=True)  124 us
    psum x4, blocking collectives, layer_statistics(): lax.psum((jnp.sum(hidden_state, -1), jnp.sum(hidden_state * hidden_state,...  75.1 us
    psum x4, blocking collectives, norm_back(): lax.psum((jnp.sum(d_hat, -1), jnp.sum(d_hat * normed, -1)), 'tensor')  69.8 us
    all_gather x2, waiting for transfers between devices, fetch_weights(): lax.all_gather(pieces[2], 'dp', axis=0, tiled=True)  49.6 us
  transfers between devices with their start and end apart: 26, of which 25 were waited for; matrix products, arithmetic and copies ran while one was open for 10% of the time, Pallas kernels for 0%

commit v1 on v0

--- a/solution.py
+++ b/solution.py
@@ -19,6 +19,11 @@
 CONTRACT_FIRST = (((0,), (0,)), ((), ()))
 
 
+def exchange_gather(x, axis, dim):
+    stack = jnp.stack([x] * lax.axis_size(axis))
+    return jnp.concatenate(lax.all_to_all(stack, axis, 0, 0), axis=dim)
+
+
 def as_sent(shard):
     return jax.tree.map(lambda a: a.astype(jnp.bfloat16) if a.dtype == jnp.float32 else a, shard)
 
@@ -54,7 +59,7 @@
 
 
 def share_features(local_rows):
-    return lax.all_gather(local_rows, "tensor", axis=2, tiled=True)
+    return exchange_gather(local_rows, "tensor", 2)
 
 
 def sum_branch(partial_rows):

time: 1680 us -> 1610 us (0.958)
  waiting for transfers between devices: 1080 us -> 966 us
  local copies, waits for them, and re-layouts: 148 us -> 179 us
  starting transfers between devices: 2.52 us -> 24.2 us
    all_gather x4 -> x0, waiting for transfers between devices: 170 us -> none  [share_features(): return lax.all_gather(local_rows, 'tensor', axis=2, tiled=True)]
    all_to_all x0 -> x4, waiting for transfers between devices: none -> 148 us  [exchange_gather(): return jnp.concatenate(lax.all_to_all(stack, axis, 0, 0), axis=dim)]
    all_gather x2, waiting for transfers between devices: 45.5 us -> 0.01 us  [fetch_weights(): lax.all_gather(pieces[0], 'dp', axis=0, tiled=True)]
    all_gather x2, waiting for transfers between devices: 49.6 us -> 13.7 us  [fetch_weights(): lax.all_gather(pieces[2], 'dp', axis=0, tiled=True)]
    all_gather x2, waiting for transfers between devices: 45.9 us -> 22.9 us  [fetch_weights(): lax.all_gather(pieces[3], 'dp', axis=0, tiled=True)]
    all_to_all x0 -> x4, starting transfers between devices: none -> 22.6 us  [exchange_gather(): return jnp.concatenate(lax.all_to_all(stack, axis, 0, 0), axis=dim)]
    another operation x0 -> x6, local copies, waits for them, and re-layouts: none -> 21.4 us  [the longest x2 10.9 us: on_device(): first_normalized = share_features((first_centered_scaled * vector_rows[0]...]
    all_gather x4, waiting for transfers between devices: 144 us -> 161 us  [share_grads(): return lax.all_gather(local_rows, 'tensor', axis=2, tiled=True)]
  transfers between devices with their start and end apart: 26 -> 26, of which waited for: 25 -> 21; matrix products, arithmetic and copies ran while one was open for 10% -> 11% of each run, Pallas kernels for 0% -> 0%
where the time goes in v1:
time: 1610 us; the launch traced here: 1600 us
  waiting for transfers between devices  966 us (60%)
  blocking collectives  188 us (12%)
  local copies, waits for them, and re-layouts  179 us (11%)
  matrix products  160 us (10%)
  other arithmetic  68.2 us (4%)
  starting transfers between devices  24.2 us (2%)
  between operations  16.5 us (1%)
    reduce_scatter x4, waiting for transfers between devices, sum_branch(): lax.psum_scatter(partial_rows, 'tensor', scatter_dimension=2, tiled=True)  319 us
    reduce_scatter x4, waiting for transfers between devices, sum_inputs(): lax.psum_scatter(partial_rows.astype(jnp.bfloat16), 'tensor', scatter_dim...  176 us
    all_gather x4, waiting for transfers between devices, share_grads(): return lax.all_gather(local_rows, 'tensor', axis=2, tiled=True)  161 us
    all_to_all x4, waiting for transfers between devices, exchange_gather(): return jnp.concatenate(lax.all_to_all(stack, axis, 0, 0), axis=dim)  148 us
    reduce_scatter x4, waiting for transfers between devices, on_device(): lax.psum_scatter(as_sent(stacked), 'dp', scatter_dimension=1, tiled=True)  124 us
    psum x4, blocking collectives, layer_statistics(): lax.psum((jnp.sum(hidden_state, -1), jnp.sum(hidden_state * hidden_state,...  75 us
    psum x4, blocking collectives, norm_back(): lax.psum((jnp.sum(d_hat, -1), jnp.sum(d_hat * normed, -1)), 'tensor')  69.8 us
    unnamed x192, local copies, waits for them, and re-layouts  33.1 us
  transfers between devices with their start and end apart: 26, of which 21 were waited for; matrix products, arithmetic and copies ran while one was open for 11% of the time, Pallas kernels for 0%

profile of v1, /device:TPU:0, one launch (start us, length us, event | category | flops | bytes accessed | tf_op | source)
XLA Modules:
  0.0 1602.4 jit_solution(5338226936141937372)
XLA Ops:
  9.8 20.5 %all-reduce.8 = (f32[2,577]{1,0:T(2,128)S(1)}, f32[2,577]{1,0:T(2,128)S(1)}) all-reduce(f32[2,577]{1,0:T(2,128)S(1)} %get-tuple-element.143, f32[2,577]{1,0:T(2,128)S(1)} %get-tuple-element.142), channel_id=1, replica_groups=mesh['dp'=8,'tensor'=4] {'tensor'}, use_global_device_ids=true, to_apply=%region_3.0 | all-reduce | flops 2308 | bytes 18464 | tf_op jit(solution)/shard_map/psum | solution.py:43
  41.3 9.9 all-gather.1
  51.1 39.4 %all-to-all-done = bf16[4,2,577,256]{3,1,2,0:T(2,128)(2,1)} async-done(((bf16[4,2,577,256]{3,1,2,0:T(2,128)(2,1)}), bf16[4,2,577,256]{3,1,2,0:T(2,128)(2,1)}, u32[]{:S(2)}, u32[]{:S(2)}) %all-to-all-start) | async-done | bytes 2363424 | tf_op jit(solution)/shard_map/all_to_all | solution.py:24
  94.6 5.4 reshape.311
  135.9 83.5 %reduce-scatter.13.cloned.1.call-done = f32[2,577,256]{2,1,0:T(8,128)} async-done(((f32[2,577,1024]{2,1,0:T(8,128)}), f32[2,577,256]{2,1,0:T(8,128)}) %reduce-scatter.13.cloned.1.call-update) | async-done | bytes 1181712 | tf_op jit(solution)/shard_map/reduce_scatter | solution.py:66
  221.1 18.0 %all-reduce.7 = (f32[2,577]{1,0:T(2,128)S(1)}, f32[2,577]{1,0:T(2,128)S(1)}) all-reduce(f32[2,577]{1,0:T(2,128)S(1)} %get-tuple-element.133, f32[2,577]{1,0:T(2,128)S(1)} %get-tuple-element.132), channel_id=1, replica_groups=mesh['dp'=8,'tensor'=4] {'tensor'}, use_global_device_ids=true, to_apply=%region_10.0 | all-reduce | flops 2308 | bytes 18464 | tf_op jit(solution)/shard_map/psum | solution.py:43
  248.9 49.5 %all-to-all-done.1 = bf16[4,2,577,256]{3,1,2,0:T(2,128)(2,1)} async-done(((bf16[4,2,577,256]{3,1,2,0:T(2,128)(2,1)}), bf16[4,2,577,256]{3,1,2,0:T(2,128)(2,1)}, u32[]{:S(2)}, u32[]{:S(2)}) %all-to-all-start.1) | async-done | bytes 2363424 | tf_op jit(solution)/shard_map/all_to_all | solution.py:24
  304.2 7.2 multiply_convert_fusion.3
  311.4 7.1 fusion.16
  318.5 4.9 reshape.291
  323.5 85.6 %reduce-scatter.15.cloned.1.call-done = f32[2,577,256]{2,1,0:T(8,128)} async-done(((f32[2,577,1024]{2,1,0:T(8,128)}), f32[2,577,256]{2,1,0:T(8,128)}) %reduce-scatter.15.cloned.1.call-update) | async-done | bytes 1181712 | tf_op jit(solution)/shard_map/reduce_scatter | solution.py:66
  410.8 18.0 %all-reduce.6 = (f32[2,577]{1,0:T(2,128)S(1)}, f32[2,577]{1,0:T(2,128)S(1)}) all-reduce(f32[2,577]{1,0:T(2,128)S(1)} %get-tuple-element.131, f32[2,577]{1,0:T(2,128)S(1)} %get-tuple-element.130), channel_id=1, replica_groups=mesh['dp'=8,'tensor'=4] {'tensor'}, use_global_device_ids=true, to_apply=%region_15.0 | all-reduce | flops 2308 | bytes 18464 | tf_op jit(solution)/shard_map/psum | solution.py:43
  437.6 11.0 all-gather.5
  448.6 38.8 %all-to-all-done.2 = bf16[4,2,577,256]{3,1,2,0:T(2,128)(2,1)} async-done(((bf16[4,2,577,256]{3,1,2,0:T(2,128)(2,1)}), bf16[4,2,577,256]{3,1,2,0:T(2,128)(2,1)}, u32[]{:S(2)}, u32[]{:S(2)}) %all-to-all-start.2) | async-done | bytes 2363424 | tf_op jit(solution)/shard_map/all_to_all | solution.py:24
  491.4 5.4 reshape.313
  535.8 81.8 %reduce-scatter.17.cloned.1.call-done = f32[2,577,256]{2,1,0:T(8,128)} async-done(((f32[2,577,1024]{2,1,0:T(8,128)}), f32[2,577,256]{2,1,0:T(8,128)}) %reduce-scatter.17.cloned.1.call-update) | async-done | bytes 1181712 | tf_op jit(solution)/shard_map/reduce_scatter | solution.py:66
  620.0 18.6 %all-reduce.5 = (f32[2,577]{1,0:T(2,128)S(1)}, f32[2,577]{1,0:T(2,128)S(1)}) all-reduce(f32[2,577]{1,0:T(2,128)S(1)} %get-tuple-element.129, f32[2,577]{1,0:T(2,128)S(1)} %get-tuple-element.128), channel_id=1, replica_groups=mesh['dp'=8,'tensor'=4] {'tensor'}, use_global_device_ids=true, to_apply=%region_22.0 | all-reduce | flops 2308 | bytes 18464 | tf_op jit(solution)/shard_map/psum | solution.py:43
  643.4 8.8 all-to-all-start.3
  653.0 45.2 %all-gather.19.cloned.1.call-done = bf16[2,577,1024]{2,1,0:T(8,128)(2,1)} async-done(((bf16[2,577,256]{2,1,0:T(8,128)(2,1)}), bf16[2,577,1024]{2,1,0:T(8,128)(2,1)}) %all-gather.19.cloned.1.call-update) | async-done | bytes 2363408 | tf_op jit(solution)/shard_map/all_gather | solution.py:70
  701.7 20.2 %all-to-all-done.3 = bf16[4,2,577,256]{3,1,2,0:T(2,128)(2,1)} async-done(((bf16[4,2,577,256]{3,1,2,0:T(2,128)(2,1)}), bf16[4,2,577,256]{3,1,2,0:T(2,128)(2,1)}, u32[]{:S(2)}, u32[]{:S(2)}) %all-to-all-start.3) | async-done | bytes 2363424 | tf_op jit(solution)/shard_map/all_to_all | solution.py:24
  727.4 13.7 all-gather.35.cloned.1.call-done
  741.1 7.2 multiply_convert_fusion.2
  748.4 22.9 %all-gather.37.cloned.1.call-done = bf16[1,1024,1024]{2,1,0:T(8,128)(2,1)} async-done(((bf16[1,128,1024]{2,1,0:T(8,128)(2,1)}), bf16[1,1024,1024]{2,1,0:T(8,128)(2,1)}) %all-gather.37.cloned.1.call-update) | async-done | bytes 2097168 | tf_op jit(solution)/shard_map/all_gather | solution.py:90
  771.3 7.1 fusion.135
  787.4 7.2 fusion.11
  794.6 5.0 reshape.294
  799.7 36.1 %reduce-scatter.21.cloned.1.call-done = bf16[2,577,256]{2,1,0:T(8,128)(2,1)} async-done(((bf16[2,577,1024]{2,1,0:T(8,128)(2,1)}), bf16[2,577,256]{2,1,0:T(8,128)(2,1)}) %reduce-scatter.21.cloned.1.call-update) | async-done | bytes 590864 | tf_op jit(solution)/shard_map/reduce_scatter | solution.py:74
  838.0 18.0 %all-reduce.4 = (f32[2,577]{1,0:T(2,128)S(1)}, f32[2,577]{1,0:T(2,128)S(1)}) all-reduce(f32[2,577]{1,0:T(2,128)S(1)} %get-tuple-element.123, f32[2,577]{1,0:T(2,128)S(1)} %get-tuple-element.136), channel_id=1, replica_groups=mesh['dp'=8,'tensor'=4] {'tensor'}, use_global_device_ids=true, to_apply=%region_28.0 | all-reduce | flops 2308 | bytes 18464 | tf_op jit(solution)/shard_map/psum | solution.py:54
  856.0 68.1 %reduce-scatter.19.cloned.1.call-done = f32[2,577,256]{2,1,0:T(8,128)} async-done(((f32[2,577,1024]{2,1,0:T(8,128)}), f32[2,577,256]{2,1,0:T(8,128)}) %reduce-scatter.19.cloned.1.call-update) | async-done | bytes 1181712 | tf_op jit(solution)/shard_map/reduce_scatter | solution.py:66
  929.5 51.5 %all-gather.21.cloned.1.call-done = bf16[2,577,1024]{2,1,0:T(8,128)(2,1)} async-done(((bf16[2,577,256]{2,1,0:T(8,128)(2,1)}), bf16[2,577,1024]{2,1,0:T(8,128)(2,1)}) %all-gather.21.cloned.1.call-update) | async-done | bytes 2363408 | tf_op jit(solution)/shard_map/all_gather | solution.py:70
  994.8 8.6 multiply_convert_fusion.1
  1042.3 46.6 %reduce-scatter.23.cloned.1.call-done = bf16[2,577,256]{2,1,0:T(8,128)(2,1)} async-done(((bf16[2,577,1024]{2,1,0:T(8,128)(2,1)}), bf16[2,577,256]{2,1,0:T(8,128)(2,1)}) %reduce-scatter.23.cloned.1.call-update) | async-done | bytes 590864 | tf_op jit(solution)/shard_map/reduce_scatter | solution.py:74
  1090.6 17.2 %all-reduce.3 = (f32[2,577]{1,0:T(2,128)S(1)}, f32[2,577]{1,0:T(2,128)S(1)}) all-reduce(f32[2,577]{1,0:T(2,128)S(1)} %get-tuple-element.125, f32[2,577]{1,0:T(2,128)S(1)} %get-tuple-element.135), channel_id=1, replica_groups=mesh['dp'=8,'tensor'=4] {'tensor'}, use_global_device_ids=true, to_apply=%region_34.0 | all-reduce | flops 2308 | bytes 18464 | tf_op jit(solution)/shard_map/psum | solution.py:54
  1112.4 49.1 %all-gather.23.cloned.1.call-done = bf16[2,577,1024]{2,1,0:T(8,128)(2,1)} async-done(((bf16[2,577,256]{2,1,0:T(8,128)(2,1)}), bf16[2,577,1024]{2,1,0:T(8,128)(2,1)}) %all-gather.23.cloned.1.call-update) | async-done | bytes 2363408 | tf_op jit(solution)/shard_map/all_gather | solution.py:70
  1165.1 7.1 fusion.136
  1181.2 46.6 %reduce-scatter.25.cloned.1.call-done = bf16[2,577,256]{2,1,0:T(8,128)(2,1)} async-done(((bf16[2,577,1024]{2,1,0:T(8,128)(2,1)}), bf16[2,577,256]{2,1,0:T(8,128)(2,1)}) %reduce-scatter.25.cloned.1.call-update) | async-done | bytes 590864 | tf_op jit(solution)/shard_map/reduce_scatter | solution.py:74
  1230.2 17.2 %all-reduce.2 = (f32[2,577]{1,0:T(2,128)S(1)}, f32[2,577]{1,0:T(2,128)S(1)}) all-reduce(f32[2,577]{1,0:T(2,128)S(1)} %get-tuple-element.121, f32[2,577]{1,0:T(2,128)S(1)} %get-tuple-element.137), channel_id=1, replica_groups=mesh['dp'=8,'tensor'=4] {'tensor'}, use_global_device_ids=true, to_apply=%region_39.0 | all-reduce | flops 2308 | bytes 18464 | tf_op jit(solution)/shard_map/psum | solution.py:54
  1252.0 5.5 convert_bitcast_fusion.2
  1263.3 5.5 convert_bitcast_fusion
  1285.8 15.1 all-gather.25.cloned.1.call-done
  1313.5 6.8 multiply_convert_fusion
  1322.9 7.4 fusion.125
  1365.9 42.0 %reduce-scatter.35.cloned.1.call-done = bf16[2,128,1024]{2,1,0:T(8,128)(2,1)} async-done(((bf16[2,1024,1024]{2,1,0:T(8,128)(2,1)}), bf16[2,128,1024]{2,1,0:T(8,128)(2,1)}) %reduce-scatter.35.cloned.1.call-update) | async-done | bytes 524304 | tf_op jit(solution)/shard_map/reduce_scatter | solution.py:349
  1412.7 34.8 %reduce-scatter.31.cloned.1.call-done = bf16[2,128,256]{2,1,0:T(8,128)(2,1)} async-done(((bf16[2,1024,256]{2,1,0:T(8,128)(2,1)}), bf16[2,128,256]{2,1,0:T(8,128)(2,1)}) %reduce-scatter.31.cloned.1.call-update) | async-done | bytes 131088 | tf_op jit(solution)/shard_map/reduce_scatter | solution.py:349
  1450.3 46.7 %reduce-scatter.29.cloned.1.call-done = bf16[2,128,3,256]{3,1,2,0:T(8,128)(2,1)} async-done(((bf16[2,1024,3,256]{3,1,2,0:T(8,128)(2,1)}), bf16[2,128,3,256]{3,1,2,0:T(8,128)(2,1)}) %reduce-scatter.29.cloned.1.call-update) | async-done | bytes 393232 | tf_op jit(solution)/shard_map/reduce_scatter | solution.py:349
  1501.0 46.6 %reduce-scatter.27.cloned.1.call-done = bf16[2,577,256]{2,1,0:T(8,128)(2,1)} async-done(((bf16[2,577,1024]{2,1,0:T(8,128)(2,1)}), bf16[2,577,256]{2,1,0:T(8,128)(2,1)}) %reduce-scatter.27.cloned.1.call-update) | async-done | bytes 590864 | tf_op jit(solution)/shard_map/reduce_scatter | solution.py:74
  1549.5 17.3 %all-reduce.1 = (f32[2,577]{1,0:T(2,128)S(1)}, f32[2,577]{1,0:T(2,128)S(1)}) all-reduce(f32[2,577]{1,0:T(2,128)S(1)} %get-tuple-element.127, f32[2,577]{1,0:T(2,128)S(1)} %get-tuple-element.134), channel_id=1, replica_groups=mesh['dp'=8,'tensor'=4] {'tensor'}, use_global_device_ids=true, to_apply=%region_45.0 | all-reduce | flops 2308 | bytes 18464 | tf_op jit(solution)/shard_map/psum | solution.py:54
  1570.4 22.4 %all-reduce = (f32[2,8,256]{2,1,0:T(8,128)S(1)}, f32[2,1024]{1,0:T(2,128)S(1)}) all-reduce(f32[2,8,256]{2,1,0:T(8,128)S(1)} %pad_maximum_fusion.9, f32[2,1024]{1,0:T(2,128)S(1)} %pad_maximum_fusion.11), channel_id=1, replica_groups=mesh['dp'=8,'tensor'=4] {'dp'}, use_global_device_ids=true, to_apply=%region_66.0 | all-reduce | flops 6144 | bytes 49152 | tf_op jit(solution)/shard_map/psum | solution.py:351
  (405 shorter events, 327.5 us)
Async XLA Ops:
  8.3 230.9 %copy-start.68 = (f32[1,1,256]{2,1,0:T(1,128)}, f32[1,1,256]{2,1,0:T(1,128)S(1)}, u32[]{:S(2)}) copy-start(f32[1,1,256]{2,1,0:T(1,128)S(1)} %get-tuple-element.229) | copy-start | bytes 3076
  35.4 55.1 %all-to-all-start = ((bf16[4,2,577,256]{3,1,2,0:T(2,128)(2,1)}), bf16[4,2,577,256]{3,1,2,0:T(2,128)(2,1)}, u32[]{:S(2)}, u32[]{:S(2)}) async-start(bf16[4,2,577,256]{3,1,2,0:T(2,128)(2,1)} %stack.217), calls=%async_computation | async-start | bytes 4726784 | tf_op jit(solution)/shard_map/all_to_all | solution.py:24
  40.1 59.9 %all-gather.27.cloned.1.call-start = ((), (), s32[]{:S(2)}) async-start(), calls=%async_computation.32 | async-start | bytes 1769472 | tf_op jit(solution)/shard_map/all_gather | solution.py:87
  41.0 178.4 %reduce-scatter.13.cloned.1.call-start = ((), (), s32[]{:S(2)}) async-start(), calls=%async_computation.16 | async-start | bytes 5980160 | tf_op jit(solution)/shard_map/reduce_scatter | solution.py:66
  41.1 78.9 %copy-start.61 = (f32[4,64]{1,0:T(4,128)}, f32[4,64]{1,0:T(4,128)S(1)}, u32[]{:S(2)}) copy-start(f32[4,64]{1,0:T(4,128)S(1)} %add.365) | copy-start | bytes 3076
  41.2 84.8 %copy-start.63 = (f32[4,64]{1,0:T(4,128)}, f32[4,64]{1,0:T(4,128)S(1)}, u32[]{:S(2)}) copy-start(f32[4,64]{1,0:T(4,128)S(1)} %add.362) | copy-start | bytes 3076
  51.1 79.6 %copy-start.38 = (bf16[1,1024,256]{2,1,0:T(8,128)(2,1)}, bf16[1,1024,256]{2,1,0:T(8,128)(2,1)S(1)}, u32[]{:S(2)}) copy-start(bf16[1,1024,256]{2,1,0:T(8,128)(2,1)S(1)} %all-gather.1) | copy-start | bytes 1572868
  133.8 85.6 %copy-start.5 = (bf16[2,577,256]{2,0,1:T(2,128)(2,1)S(1)}, bf16[2,577,256]{2,0,1:T(2,128)(2,1)}, u32[]{:S(2)}) copy-start(bf16[2,577,256]{2,0,1:T(2,128)(2,1)} %param.15) | copy-start | bytes 1772548
  133.8 170.4 %all-gather.29.cloned.1.call-start = ((), (), s32[]{:S(2)}) async-start(), calls=%async_computation.33 | async-start | bytes 2359296 | tf_op jit(solution)/shard_map/all_gather | solution.py:89
  243.2 55.3 %all-to-all-start.1 = ((bf16[4,2,577,256]{3,1,2,0:T(2,128)(2,1)}), bf16[4,2,577,256]{3,1,2,0:T(2,128)(2,1)}, u32[]{:S(2)}, u32[]{:S(2)}) async-start(bf16[4,2,577,256]{3,1,2,0:T(2,128)(2,1)} %stack.218), calls=%async_computation.2 | async-start | bytes 4726784 | tf_op jit(solution)/shard_map/all_to_all | solution.py:24
  247.9 63.5 %all-gather.31.cloned.1.call-start = ((), (), s32[]{:S(2)}) async-start(), calls=%async_computation.34 | async-start | bytes 2359296 | tf_op jit(solution)/shard_map/all_gather | solution.py:90
  248.8 160.2 %reduce-scatter.15.cloned.1.call-start = ((), (), s32[]{:S(2)}) async-start(), calls=%async_computation.17 | async-start | bytes 5980160 | tf_op jit(solution)/shard_map/reduce_scatter | solution.py:66
  432.3 55.1 %all-to-all-start.2 = ((bf16[4,2,577,256]{3,1,2,0:T(2,128)(2,1)}), bf16[4,2,577,256]{3,1,2,0:T(2,128)(2,1)}, u32[]{:S(2)}, u32[]{:S(2)}) async-start(bf16[4,2,577,256]{3,1,2,0:T(2,128)(2,1)} %stack.219), calls=%async_computation.4 | async-start | bytes 4726784 | tf_op jit(solution)/shard_map/all_to_all | solution.py:24
  436.8 60.1 %all-gather.33.cloned.1.call-start = ((), (), s32[]{:S(2)}) async-start(), calls=%async_computation.35 | async-start | bytes 1769472 | tf_op jit(solution)/shard_map/all_gather | solution.py:87
  437.4 180.3 %reduce-scatter.17.cloned.1.call-start = ((), (), s32[]{:S(2)}) async-start(), calls=%async_computation.18 | async-start | bytes 5980160 | tf_op jit(solution)/shard_map/reduce_scatter | solution.py:66
  532.1 166.2 %all-gather.19.cloned.1.call-start = ((), (), s32[]{:S(2)}) async-start(), calls=%async_computation.20 | async-start | bytes 2990080 | tf_op jit(solution)/shard_map/all_gather | solution.py:70
  532.8 391.3 %copy-start.75 = (f32[2]{0:T(128)}, f32[2]{0:T(128)S(1)}, u32[]{:S(2)}) copy-start(f32[2]{0:T(128)S(1)} %add_convert_fusion.15) | copy-start | bytes 28
  535.1 206.0 %all-gather.35.cloned.1.call-start = ((), (), s32[]{:S(2)}) async-start(), calls=%async_computation.36 | async-start | bytes 2359296 | tf_op jit(solution)/shard_map/all_gather | solution.py:89
  643.4 78.5 %all-to-all-start.3 = ((bf16[4,2,577,256]{3,1,2,0:T(2,128)(2,1)}), bf16[4,2,577,256]{3,1,2,0:T(2,128)(2,1)}, u32[]{:S(2)}, u32[]{:S(2)}) async-start(bf16[4,2,577,256]{3,1,2,0:T(2,128)(2,1)} %stack.220), calls=%async_computation.6 | async-start | bytes 4726784 | tf_op jit(solution)/shard_map/all_to_all | solution.py:24
  652.2 119.0 %all-gather.37.cloned.1.call-start = ((), (), s32[]{:S(2)}) async-start(), calls=%async_computation.37 | async-start | bytes 2359296 | tf_op jit(solution)/shard_map/all_gather | solution.py:90
  652.8 183.0 %reduce-scatter.21.cloned.1.call-start = ((), (), s32[]{:S(2)}) async-start(), calls=%async_computation.21 | async-start | bytes 2990080 | tf_op jit(solution)/shard_map/reduce_scatter | solution.py:74
  787.4 136.7 %reduce-scatter.19.cloned.1.call-start = ((), (), s32[]{:S(2)}) async-start(), calls=%async_computation.19 | async-start | bytes 5980160 | tf_op jit(solution)/shard_map/reduce_scatter | solution.py:66
  799.6 181.4 %all-gather.21.cloned.1.call-start = ((), (), s32[]{:S(2)}) async-start(), calls=%async_computation.22 | async-start | bytes 2990080 | tf_op jit(solution)/shard_map/all_gather | solution.py:70
  929.5 159.4 %reduce-scatter.23.cloned.1.call-start = ((), (), s32[]{:S(2)}) async-start(), calls=%async_computation.23 | async-start | bytes 2990080 | tf_op jit(solution)/shard_map/reduce_scatter | solution.py:74
  1042.2 119.3 %all-gather.23.cloned.1.call-start = ((), (), s32[]{:S(2)}) async-start(), calls=%async_computation.24 | async-start | bytes 2990080 | tf_op jit(solution)/shard_map/all_gather | solution.py:70
  1112.3 115.5 %reduce-scatter.25.cloned.1.call-start = ((), (), s32[]{:S(2)}) async-start(), calls=%async_computation.25 | async-start | bytes 2990080 | tf_op jit(solution)/shard_map/reduce_scatter | solution.py:74
  1181.2 46.7 %copy-start.53 = (f32[2,577]{1,0:T(2,128)S(1)}, f32[2,577]{1,0:T(2,128)}, u32[]{:S(2)}) copy-start(f32[2,577]{1,0:T(2,128)} %copy-done.52) | copy-start | bytes 13852
  1181.2 46.7 %copy-start.55 = (f32[2,577]{1,0:T(2,128)S(1)}, f32[2,577]{1,0:T(2,128)}, u32[]{:S(2)}) copy-start(f32[2,577]{1,0:T(2,128)} %copy-done.54) | copy-start | bytes 13852
  1181.2 46.7 %copy-start.69 = (f32[1,1,256]{2,1,0:T(1,128)S(1)}, f32[1,1,256]{2,1,0:T(1,128)}, u32[]{:S(2)}) copy-start(f32[1,1,256]{2,1,0:T(1,128)} %copy-done.68) | copy-start | bytes 3076
  1181.2 66.3 %copy-start.16 = (f32[2,577,256]{2,1,0:T(8,128)S(1)}, f32[2,577,256]{2,1,0:T(8,128)}, u32[]{:S(2)}) copy-start(f32[2,577,256]{2,1,0:T(8,128)} %copy-done.15) | copy-start | bytes 3545092
  1181.2 119.7 %all-gather.25.cloned.1.call-start = ((), (), s32[]{:S(2)}) async-start(), calls=%async_computation.26 | async-start | bytes 2990080 | tf_op jit(solution)/shard_map/all_gather | solution.py:70
  1251.8 107.9 %reduce-scatter.33.cloned.1.call-start = ((), (), s32[]{:S(2)}) async-start(), calls=%async_computation.30 | async-start | bytes 4718592 | tf_op jit(solution)/shard_map/reduce_scatter | solution.py:349
  1263.2 144.8 %reduce-scatter.35.cloned.1.call-start = ((), (), s32[]{:S(2)}) async-start(), calls=%async_computation.31 | async-start | bytes 4718592 | tf_op jit(solution)/shard_map/reduce_scatter | solution.py:349
  1274.4 173.2 %reduce-scatter.31.cloned.1.call-start = ((), (), s32[]{:S(2)}) async-start(), calls=%async_computation.29 | async-start | bytes 1179648 | tf_op jit(solution)/shard_map/reduce_scatter | solution.py:349
  1330.3 166.7 %reduce-scatter.29.cloned.1.call-start = ((), (), s32[]{:S(2)}) async-start(), calls=%async_computation.28 | async-start | bytes 3538944 | tf_op jit(solution)/shard_map/reduce_scatter | solution.py:349
  1346.6 201.0 %reduce-scatter.27.cloned.1.call-start = ((), (), s32[]{:S(2)}) async-start(), calls=%async_computation.27 | async-start | bytes 2990080 | tf_op jit(solution)/shard_map/reduce_scatter | solution.py:74
  1364.5 43.5 %copy-start.24 = (f32[2,2,128,1024]{3,2,1,0:T(8,128)S(1)}, f32[2,2,128,1024]{3,2,1,0:T(8,128)}, u32[]{:S(2)}) copy-start(f32[2,2,128,1024]{3,2,1,0:T(8,128)} %param.27) | copy-start | bytes 6291460
  1411.1 36.5 %copy-start.42 = (f32[2,2,128,256]{3,2,1,0:T(8,128)S(1)}, f32[2,2,128,256]{3,2,1,0:T(8,128)}, u32[]{:S(2)}) copy-start(f32[2,2,128,256]{3,2,1,0:T(8,128)} %param.25) | copy-start | bytes 1572868
  1411.1 37.4 %copy-start.45 = (f32[2,128,256]{2,1,0:T(8,128)S(1)}, f32[2,128,256]{2,1,0:T(8,128)}, u32[]{:S(2)}) copy-start(f32[2,128,256]{2,1,0:T(8,128)} %param.19) | copy-start | bytes 786436
  1412.6 84.5 %copy-start.30 = (f32[2,2,128,3,256]{4,2,3,1,0:T(8,128)S(1)}, f32[2,2,128,3,256]{4,2,3,1,0:T(8,128)}, u32[]{:S(2)}) copy-start(f32[2,2,128,3,256]{4,2,3,1,0:T(8,128)} %param.24) | copy-start | bytes 4718596
  1448.5 49.7 %copy-start.43 = (f32[2,128,256]{2,1,0:T(8,128)}, f32[2,128,256]{2,1,0:T(8,128)S(1)}, u32[]{:S(2)}) copy-start(f32[2,128,256]{2,1,0:T(8,128)S(1)} %get-tuple-element.171) | copy-start | bytes 786436
  1449.5 48.7 %copy-start.32 = (f32[2,128,3,256]{3,1,2,0:T(8,128)S(1)}, f32[2,128,3,256]{3,1,2,0:T(8,128)}, u32[]{:S(2)}) copy-start(f32[2,128,3,256]{3,1,2,0:T(8,128)} %param.18) | copy-start | bytes 2359300
  1499.7 47.9 %copy-start.6 = (bf16[2,577,256]{2,0,1:T(2,128)(2,1)S(1)}, bf16[2,577,256]{2,0,1:T(2,128)(2,1)}, u32[]{:S(2)}) copy-start(bf16[2,577,256]{2,0,1:T(2,128)(2,1)} %param.15) | copy-start | bytes 1772548
  1499.7 47.9 %copy-start.57 = (f32[2,577]{1,0:T(2,128)S(1)}, f32[2,577]{1,0:T(2,128)}, u32[]{:S(2)}) copy-start(f32[2,577]{1,0:T(2,128)} %copy-done.56) | copy-start | bytes 13852
  1499.7 47.9 %copy-start.59 = (f32[2,577]{1,0:T(2,128)S(1)}, f32[2,577]{1,0:T(2,128)}, u32[]{:S(2)}) copy-start(f32[2,577]{1,0:T(2,128)} %copy-done.58) | copy-start | bytes 13852
  1499.7 47.9 %copy-start.73 = (f32[1,1,256]{2,1,0:T(1,128)S(1)}, f32[1,1,256]{2,1,0:T(1,128)}, u32[]{:S(2)}) copy-start(f32[1,1,256]{2,1,0:T(1,128)} %copy-done.72) | copy-start | bytes 3076
  1499.7 67.1 %copy-start.14 = (f32[2,577,256]{2,1,0:T(8,128)S(1)}, f32[2,577,256]{2,1,0:T(8,128)}, u32[]{:S(2)}) copy-start(f32[2,577,256]{2,1,0:T(8,128)} %copy-done.13) | copy-start | bytes 3545092
  1499.7 67.1 %copy-start.76 = (f32[2]{0:T(128)S(1)}, f32[2]{0:T(128)}, u32[]{:S(2)}) copy-start(f32[2]{0:T(128)} %copy-done.75) | copy-start | bytes 28
  (69 other events, 378.6 us)
Sparse Core Ops, SparseCore 0:
  43.4 26.9 all-gather.26
  133.9 85.4 reduce-scatter.12
  221.9 28.2 all-gather.28
  252.5 27.7 all-gather.30
  323.6 85.3 reduce-scatter.14
  439.8 27.1 all-gather.32
  532.2 85.3 reduce-scatter.16
  619.8 78.4 all-gather.18
  700.7 40.4 all-gather.34
  743.5 27.7 all-gather.36
  787.5 48.2 reduce-scatter.20
  838.0 86.0 reduce-scatter.18
  929.6 51.4 all-gather.20
  1042.3 46.4 reduce-scatter.22
  1112.5 49.0 all-gather.22
  1181.3 46.4 reduce-scatter.24
  1251.9 49.0 all-gather.24
  1304.1 49.2 reduce-scatter.32
  1356.8 51.0 reduce-scatter.34
  1411.6 35.9 reduce-scatter.30
  1451.0 46.0 reduce-scatter.28
  1499.4 48.2 reduce-scatter.26
